TPU v7x, 1024 devices: a whole 4x8x16 slice. The times are simulated.
1024 devices in a mesh: group: 64 (over z_lo, y), inner: 16 (over x, z_hi, core).
Axes of the slice: x: 4, y: 8, z: 16 (z_hi: 2, z_lo: 8; z = z_hi * 8 + z_lo), core: 2. Of those that a mesh axis runs over, the one named last changes fastest.
Arguments:
- tokens: bfloat16 [393216, 4096], P(('group', 'inner')), may hold values from -6 to 6
- master_weight: float32 [4096, 768], P('inner', 'group'), may hold values from -0.09375 to 0.09375
- first_moment: float32 [4096, 768], P('inner', 'group'), may hold values from -6 to 6
- second_moment: float32 [4096, 768], P('inner', 'group'), may hold values from 0.1 to 10
- gradient: float32 [4096, 768], P('inner', 'group'), may hold values from -6 to 6
- gate_weight: bfloat16 [4096, 2], P('inner'), may hold values from -0.09375 to 0.09375
- input_bias: float32 [1], replicated, may hold values from -3 to -1
- forget_bias: float32 [1], replicated, may hold values from 2 to 5
Outputs:
- new_master: float32 [4096, 768], P('inner', 'group')
- new_first: float32 [4096, 768], P('inner', 'group')
- new_second: float32 [4096, 768], P('inner', 'group')
- hidden: bfloat16 [393216, 256], P(('group', 'inner'))
All inputs are finite; a program needn't handle non-finite values.
Results may differ from a plain program's by a relative error of at most 0.012.
Values may be sent and summed in bfloat16 or wider, within the bound.
A program may use at most 32 MiB of HBM per device.

v0:
```python
import jax
import jax.numpy as jnp
from jax import lax
from jax.sharding import PartitionSpec as P

QK = 256


beta_first = 0.9
beta_second = 0.999
learn_rate = 0.001
adam_eps = 1e-08
fix_first = 1.0 - (0.9**10) ** 10
fix_second = 1.0 - (0.999**10) ** 10


def mlstm_head(sequence, projected, gate_pre, input_bias, forget_bias):
    query_rows = projected[:, :QK].astype(jnp.bfloat16)
    key_rows = projected[:, QK : 2 * QK].astype(jnp.bfloat16)
    value_rows = projected[:, 2 * QK :].astype(jnp.bfloat16)
    input_gate = gate_pre[:, 0] + input_bias[0]
    forget_log = jax.nn.log_sigmoid(gate_pre[:, 1] + forget_bias[0])
    cumulative = jnp.cumsum(forget_log)
    row_count = sequence.shape[0]
    causal = jnp.arange(row_count)[:, None] >= jnp.arange(row_count)[None, :]
    decay_log = cumulative[:, None] - cumulative[None, :] + input_gate[None, :]
    decay_matrix = jnp.exp(jnp.where(causal, decay_log, -jnp.inf))
    scores = jnp.dot(query_rows, key_rows.T, preferred_element_type=jnp.float32) * QK ** (-0.5)
    weighted = scores * decay_matrix
    normalizer = jnp.sum(weighted, axis=1)
    numerator = jnp.dot(
        weighted.astype(jnp.bfloat16), value_rows, preferred_element_type=jnp.float32
    )
    return (numerator / jnp.maximum(jnp.abs(normalizer), 1.0)[:, None]).astype(jnp.bfloat16)


def on_device(
    tokens,
    master_weight,
    first_moment,
    second_moment,
    gradient,
    gate_weight,
    input_bias,
    forget_bias,
):
    new_first = beta_first * first_moment + (1.0 - beta_first) * gradient
    new_second = beta_second * second_moment + (1.0 - beta_second) * gradient * gradient
    new_master = master_weight - learn_rate * (new_first / fix_first) / (
        jnp.sqrt(new_second / fix_second) + adam_eps
    )
    sendable = new_master.astype(jnp.bfloat16)
    secondary = lax.all_gather(sendable, "group", axis=1, tiled=True)
    projected = jnp.dot(
        tokens,
        lax.all_gather(secondary, "inner", axis=0, tiled=True),
        preferred_element_type=jnp.float32,
    )
    gate_pre = jnp.dot(
        tokens,
        lax.all_gather(gate_weight, "inner", axis=0, tiled=True),
        preferred_element_type=jnp.float32,
    )
    hidden = mlstm_head(tokens, projected, gate_pre, input_bias, forget_bias)
    return (new_master, new_first, new_second, hidden)


def solution(mesh):
    placed = (
        P(("group", "inner"), None),
        P("inner", "group"),
        P("inner", "group"),
        P("inner", "group"),
        P("inner", "group"),
        P("inner", None),
        P(),
        P(),
    )
    return jax.shard_map(
        on_device,
        mesh=mesh,
        in_specs=placed,
        out_specs=(
            P("inner", "group"),
            P("inner", "group"),
            P("inner", "group"),
            P(("group", "inner"), None),
        ),
        check_vma=False,
    )
```

profile of v0, /device:TPU:1, one launch (start us, length us, event | category | flops | bytes accessed | tf_op | source)
XLA Modules:
  0.0 430.9 jit_solution(114875617881050057)
XLA Ops:
  7.2 0.0 copy-start
  7.2 0.0 all-gather.3.cloned.1.call-start
  7.2 1.5 convert_bitcast_fusion
  8.8 224.6 %all-gather = bf16[64,12,256]{2,1,0:T(8,128)(2,1)} all-gather(bf16[1,12,256]{2,1,0:T(8,128)(2,1)S(1)} %get-tuple-element.6), channel_id=1, replica_groups=mesh['group'=64,'inner'=16] {'group'}, dimensions={0}, use_global_device_ids=true | all-gather | bytes 399360 | tf_op jit(solution)/shard_map/all_gather | solution.py:53
  233.4 1.9 reshape.61
  235.3 0.0 all-gather.3.cloned.1.call-update
  236.6 74.9 %all_gather.11 = bf16[4096,2]{0,1:T(2,128)(2,1)S(1)} all-gather(bf16[256,2]{0,1:T(2,128)(2,1)} %param.13), channel_id=1, replica_groups=mesh['group'=64,'inner'=16] {'inner'}, dimensions={0}, use_global_device_ids=true | all-gather | bytes 17408 | tf_op jit(solution)/shard_map/all_gather | solution.py:61
  311.4 0.0 copy-done
  311.4 0.9 fusion.18
  312.4 0.3 reduce-window.9
  312.7 0.1 slice.28
  312.8 0.1 slice_reduce_fusion
  313.0 0.1 add_bitcast_fusion
  313.0 104.1 %all-gather.3.cloned.1.call-done = bf16[4096,768]{0,1:T(8,128)(2,1)} async-done(((bf16[256,768]{0,1:T(8,128)(2,1)}), bf16[4096,768]{0,1:T(8,128)(2,1)}) %all-gather.3.cloned.1.call-update) | async-done | bytes 6291472 | tf_op jit(solution)/shard_map/all_gather | solution.py:56
  417.1 5.6 %fusion = bf16[384,768]{0,1:T(8,128)(2,1)S(1)} fusion(bf16[4096,768]{0,1:T(8,128)(2,1)} %all-gather.3.cloned.1.call-done, bf16[384,4096]{1,0:T(8,128)(2,1)S(1)} %copy-done), kind=kOutput, calls=%fused_computation.1 | convolution fusion | flops 2416214016 | bytes 10027008 | tf_op jit(solution)/shard_map/dot_general | solution.py:54
  422.7 0.3 fusion.17
  423.1 1.0 fusion.2
  (4 shorter events, 0.1 us)
Async XLA Ops:
  7.2 304.3 %copy-start = (bf16[384,4096]{1,0:T(8,128)(2,1)S(1)}, bf16[384,4096]{1,0:T(8,128)(2,1)}, u32[]{:S(2)}) copy-start(bf16[384,4096]{1,0:T(8,128)(2,1)} %param.8) | copy-start | bytes 9437188
  7.2 410.0 %all-gather.3.cloned.1.call-start = ((), (), s32[]{:S(2)}) async-start(), calls=%async_computation | async-start | bytes 6684672 | tf_op jit(solution)/shard_map/all_gather | solution.py:56
Sparse Core Ops, SparseCore 0:
  235.4 181.6 all-gather.2
where the time goes:
time: 431 us
  blocking collectives  299 us (69%)
  waiting for transfers between devices  104 us (24%)
  between operations  15.4 us (4%)
  matrix products  7.81 us (2%)
    all_gather x1, blocking collectives, on_device(): secondary = lax.all_gather(sendable, 'group', axis=1, tiled=True)  225 us
    all_gather x1, waiting for transfers between devices, on_device(): lax.all_gather(secondary, 'inner', axis=0, tiled=True)  104 us
    all_gather x1, blocking collectives, on_device(): lax.all_gather(gate_weight, 'inner', axis=0, tiled=True)  74.9 us
  transfers between devices with their start and end apart: 1, of which 1 were waited for; matrix products, arithmetic and copies ran while one was open for 0% of the time, Pallas kernels for 0%

commit v1 on v0

v1 whole, which is shorter than its diff:
```python
import functools

import jax
import jax.numpy as jnp
from jax import lax
from jax.experimental import pallas as pl
from jax.experimental.pallas import tpu as pltpu
from jax.sharding import PartitionSpec as P

MESH = pl.DeviceIdType.MESH

QK = 256
NX, NY, NZL, NZH = 4, 8, 8, 2
NZ = NZL * NZH
TOK = 384
CHUNK = 256
HALF = 128
COLS = 12
BLOCKS = NX * NZH
ROWS_A = NY * NZL * 8
ROWS_B = NZL * NY * 4
ROWS_G = 16
ROWS = ROWS_A + ROWS_B + ROWS_G

VMEM_ALL = 67_043_328

beta_first = 0.9
beta_second = 0.999
learn_rate = 0.001
adam_eps = 1e-08
fix_first = 1.0 - (0.9**10) ** 10
fix_second = 1.0 - (0.999**10) ** 10

NT = (((1,), (1,)), ((), ()))


def adam(master, first, second, gradient):
    new_first = beta_first * first + (1.0 - beta_first) * gradient
    new_second = beta_second * second + (1.0 - beta_second) * gradient * gradient
    new_master = master - learn_rate * (new_first / fix_first) / (
        jnp.sqrt(new_second / fix_second) + adam_eps
    )
    return new_master, new_first, new_second


class Sems:
    def __init__(self, send, recv):
        self.send, self.recv, self.used, self.sent = send, recv, 0, []

    def copy(self, src, dst, device):
        k = self.used
        self.used += 1
        return pltpu.make_async_remote_copy(
            src_ref=src,
            dst_ref=dst,
            send_sem=self.send.at[k],
            recv_sem=self.recv.at[k],
            device_id=device,
            device_id_type=MESH,
        )


def gather_kernel(
    tokens,
    master,
    first,
    second,
    gradient,
    gate,
    out,
    gate_out,
    state,
    gate_in,
    x,
    pa,
    y1,
    pb,
    pg,
    wt,
    acc,
    part_out,
    part_in,
    send_sem,
    recv_sem,
    local_sem,
):
    group, inner = lax.axis_index("group"), lax.axis_index("inner")
    zl, y = group // NY, group % NY
    xc, zh, core = inner // 4, (inner // 2) % 2, inner % 2
    z = zh * NZL + zl
    sems = Sems(send_sem, recv_sem)
    started = []

    def device(x_=xc, y_=y, z_=z, core_=core):
        return ((z_ % NZL) * NY + y_, x_ * 4 + (z_ // NZL) * 2 + core_)

    def at_x(r):
        return device(x_=(xc + r + NX) % NX)

    def at_y(r):
        return device(y_=(y + r + NY) % NY)

    def at_z(r):
        return device(z_=(z + r + NZ) % NZ)

    other = device(core_=1 - core)

    def go(src, dst, dev):
        c = sems.copy(src, dst, dev)
        c.start()
        started.append(c)
        return c

    loads = [
        pltpu.make_async_copy(src, dst, local_sem.at[BLOCKS + k])
        for k, (src, dst) in enumerate(
            [(ref, state.at[k]) for k, ref in enumerate((master, first, second, gradient))]
            + [(gate, gate_in)]
        )
    ]
    for c in loads:
        c.start()

    local = []
    for m in range(BLOCKS):
        c = pltpu.make_async_copy(
            tokens.at[:, pl.ds(pl.multiple_of((2 * m + core) * CHUNK, CHUNK), CHUNK)],
            x.at[pl.ds(0, TOK), pl.ds(m * CHUNK, CHUNK)],
            local_sem.at[m],
        )
        c.start()
        local.append(c)

    barrier = pltpu.get_barrier_semaphore()
    peers = (
        [at_z(r) for r in range(1, NZ)]
        + [at_y(r) for r in range(1, NY)]
        + [at_x(r) for r in range(1, NX)]
        + [other]
    )
    for peer in peers:
        pl.semaphore_signal(barrier, inc=1, device_id=peer, device_id_type=MESH)

    for c in loads:
        c.wait()
    new_master, _, _ = adam(state[0], state[1], state[2], state[3])
    pa[0, xc, zh, y, zl] = new_master[0:8, 0:HALF].astype(jnp.bfloat16)
    pa[1, xc, zh, y, zl] = new_master[0:8, HALF:].astype(jnp.bfloat16)
    y1[y] = jnp.concatenate([new_master[8:12, 0:HALF], new_master[8:12, HALF:]], axis=0).astype(
        jnp.bfloat16
    )
    gate_rows = jnp.concatenate(
        [gate_in[...].astype(jnp.float32), jnp.zeros((ROWS_G - 2, CHUNK), jnp.float32)], axis=0
    ).astype(jnp.bfloat16)
    pg[xc, zh, 0] = gate_rows[:, 0:HALF]
    pg[xc, zh, 1] = gate_rows[:, HALF:]

    pl.semaphore_wait(barrier, len(peers))

    b_y = [go(y1.at[y], y1.at[y], at_y(r)) for r in range(1, NY)]
    a_z = [
        go(pa.at[:, xc, zh, y, zl], pa.at[:, xc, zh, y, zl], at_z(r))
        for r in (8, 7, 9, 6, 10, 5, 11, 4, 12, 3, 13, 2, 14, 1, 15)
    ]
    g_z = go(pg.at[xc, zh], pg.at[xc, zh], at_z(NZL))
    given = [
        go(
            tokens.at[:, pl.ds(pl.multiple_of((2 * m + 1 - core) * CHUNK, CHUNK), CHUNK)],
            x.at[pl.ds(TOK, TOK), pl.ds(m * CHUNK, CHUNK)],
            other,
        )
        for m in range(BLOCKS)
    ]

    for c in b_y:
        c.wait_recv()
    upper = lax.broadcasted_iota(jnp.int32, (8, HALF), 0) < 4
    low, high = [], []
    for a in range(NY // 2):
        even = y1[2 * a].astype(jnp.float32)
        odd = y1[2 * a + 1].astype(jnp.float32)
        low.append(jnp.where(upper, even, pltpu.roll(odd, 4, 0)))
        high.append(jnp.where(upper, pltpu.roll(even, 4, 0), odd))
    pb[xc, zh, 0, zl] = jnp.concatenate(low, axis=0).astype(jnp.bfloat16)
    pb[xc, zh, 1, zl] = jnp.concatenate(high, axis=0).astype(jnp.bfloat16)
    b_x = [
        go(pb.at[xc, zh, :, zl], pb.at[xc, zh, :, zl], at_x(r)) for r in (2, 1, 3)
    ]
    for c in b_x:
        c.wait_recv()

    def ring(count, chunks, region, coord, neighbour):
        half = count // 2
        copies = {}

        def send(sign, step):
            parts = range(chunks)
            if step == half:
                parts = range(chunks // 2) if sign > 0 else range(chunks // 2, chunks)
            block = (coord - sign * (step - 1) + count) % count
            for k in parts:
                copies[sign, step, k] = go(region(block, k), region(block, k), neighbour(sign))

        def advance(step):
            for k in range(chunks):
                for sign in (1, -1):
                    if (sign, step, k) in copies:
                        copies[sign, step, k].wait_recv()
                        last = step + 1 == half
                        if step < half and (not last or (k < chunks // 2) == (sign > 0)):
                            block = (coord - sign * step + count) % count
                            copies[sign, step + 1, k] = go(
                                region(block, k), region(block, k), neighbour(sign)
                            )

        send(1, 1)
        send(-1, 1)
        return advance

    z_ring = ring(
        NZ,
        2,
        lambda b, k: pb.at[pl.ds(2 * k, 2), b // NZL, :, b % NZL],
        z,
        at_z,
    )

    for c in a_z:
        c.wait_recv()
    a_x = [go(pa.at[0, xc, :, y], pa.at[0, xc, :, y], at_x(r)) for r in (2, 1, 3)]
    a_y = [go(pa.at[1, xc, :, y], pa.at[1, xc, :, y], at_y(r)) for r in (4, 3, 5, 2, 6, 1, 7)]
    g_z.wait_recv()
    g_x = [go(pg.at[xc], pg.at[xc], at_x(r)) for r in (2, 1, 3)]

    z_ring(1)
    for c in a_x:
        c.wait_recv()
    y_ring = ring(NY, 4, lambda b, k: pa.at[0, k, :, b], y, at_y)
    z_ring(2)
    y_ring(1)
    for c in a_y:
        c.wait_recv()
    x_ring = ring(NX, 4, lambda b, k: pa.at[1, b, k // 2, pl.ds(4 * (k % 2), 4)], xc, at_x)
    z_ring(3)
    y_ring(2)
    z_ring(4)
    x_ring(1)
    y_ring(3)
    z_ring(5)
    y_ring(4)
    z_ring(6)
    x_ring(2)
    z_ring(7)
    z_ring(8)
    for c in g_x:
        c.wait_recv()
    for c in local:
        c.wait()
    for c in given:
        c.wait_recv()

    for m in range(BLOCKS):
        mx, mz = m // 2, m % 2
        for kh in range(2):
            lanes = pl.ds(m * CHUNK + kh * HALF, HALF)
            wt[0:ROWS_A, lanes] = pa[kh, mx, mz].reshape(ROWS_A, HALF)
            wt[ROWS_A : ROWS_A + ROWS_B, lanes] = pb[mx, mz, kh].reshape(ROWS_B, HALF)
            wt[ROWS_A + ROWS_B :, lanes] = pg[mx, mz, kh]

    summed = []
    for lo, hi in ((512, 784), (0, 256), (256, 512)):
        res = lax.dot_general(wt[lo:hi], x[...], NT, preferred_element_type=jnp.float32)
        acc[lo:hi] = res[:, :TOK]
        part_out[lo:hi] = res[:, TOK:]
        summed.append(go(part_out.at[pl.ds(lo, hi - lo)], part_in.at[pl.ds(lo, hi - lo)], other))
    for c in summed:
        c.wait_recv()

    gate_out[...] = acc[768:776] + part_in[768:776]
    first4 = lax.broadcasted_iota(jnp.int32, (8, TOK), 0) < 4
    for l in range(NZL):
        rows = []
        for a in range(NY // 2):
            even = ((2 * a) * NZL + l) * 8
            odd = ((2 * a + 1) * NZL + l) * 8
            mixed = ROWS_A + (l * NY + 2 * a) * 4
            t0, a1, b = (
                acc[r : r + 8] + part_in[r : r + 8] for r in (even, odd, mixed)
            )
            turned = pltpu.roll(a1, 4, 0)
            rows += [t0, jnp.where(first4, b, turned), jnp.where(first4, turned, b)]
        out[l * 96 : l * 96 + 96] = jnp.concatenate(rows, axis=0).astype(jnp.bfloat16)

    for c in started:
        c.wait_send()


def head_kernel(
    projected,
    gates,
    input_bias,
    forget_bias,
    master,
    first,
    second,
    gradient,
    new_master,
    new_first,
    new_second,
    hidden,
    state,
    updated,
    sems,
):
    loads = [
        pltpu.make_async_copy(ref, state.at[k], sems.at[k])
        for k, ref in enumerate((master, first, second, gradient))
    ]
    for c in loads:
        c.start()
    for c in loads:
        c.wait()
    updated[0], updated[1], updated[2] = adam(state[0], state[1], state[2], state[3])
    stores = [
        pltpu.make_async_copy(updated.at[k], ref, sems.at[4 + k])
        for k, ref in enumerate((new_master, new_first, new_second))
    ]
    for c in stores:
        c.start()
    pre = gates[...]
    input_gate = pre[0:1] + input_bias[0]
    forget = pre[1:2] + forget_bias[0]
    forget_log = jnp.minimum(forget, 0.0) - jnp.log1p(jnp.exp(-jnp.abs(forget)))
    t = lax.broadcasted_iota(jnp.int32, (TOK, TOK), 0)
    s = lax.broadcasted_iota(jnp.int32, (TOK, TOK), 1)
    causal = t >= s
    column = jnp.sum(jnp.where(causal, forget_log, 0.0), axis=1, keepdims=True)
    lane = lax.broadcasted_iota(jnp.int32, (8, TOK), 1)
    scan = jnp.broadcast_to(forget_log, (8, TOK))
    step = 1
    while step < TOK:
        scan = scan + jnp.where(lane >= step, pltpu.roll(scan, step, 1), 0.0)
        step *= 2
    row = scan[0:1]
    decay = jnp.exp(jnp.where(causal, column - row + input_gate, -jnp.inf))
    query = projected[0:QK].T
    scores = jnp.dot(query, projected[QK : 2 * QK], preferred_element_type=jnp.float32)
    weighted = scores * QK ** (-0.5) * decay
    normalizer = jnp.sum(weighted, axis=1, keepdims=True)
    numerator = lax.dot_general(
        weighted.astype(jnp.bfloat16),
        projected[2 * QK :],
        NT,
        preferred_element_type=jnp.float32,
    )
    hidden[...] = (numerator / jnp.maximum(jnp.abs(normalizer), 1.0)).astype(jnp.bfloat16)
    for c in stores:
        c.wait()


def on_device(
    tokens,
    master_weight,
    first_moment,
    second_moment,
    gradient,
    gate_weight,
    input_bias,
    forget_bias,
):
    state = [a.T for a in (master_weight, first_moment, second_moment, gradient)]
    vmem = pl.BlockSpec(memory_space=pltpu.VMEM)
    smem = pl.BlockSpec(memory_space=pltpu.SMEM)
    hbm = pl.BlockSpec(memory_space=pltpu.HBM)
    bf16, f32 = jnp.bfloat16, jnp.float32
    copies = 160
    projected, gates = pl.pallas_call(
        gather_kernel,
        out_shape=(
            jax.ShapeDtypeStruct((3 * QK, TOK), bf16),
            jax.ShapeDtypeStruct((8, TOK), f32),
        ),
        in_specs=[hbm] * 6,
        out_specs=(vmem, vmem),
        scratch_shapes=[
            pltpu.VMEM((4, COLS, CHUNK), f32),
            pltpu.VMEM((2, CHUNK), bf16),
            pltpu.VMEM((2 * TOK, BLOCKS * CHUNK), bf16),
            pltpu.VMEM((2, NX, NZH, NY, NZL, 8, HALF), bf16),
            pltpu.VMEM((NY, 8, HALF), bf16),
            pltpu.VMEM((NX, NZH, 2, NZL, 32, HALF), bf16),
            pltpu.VMEM((NX, NZH, 2, ROWS_G, HALF), bf16),
            pltpu.VMEM((ROWS, BLOCKS * CHUNK), bf16),
            pltpu.VMEM((ROWS, TOK), f32),
            pltpu.VMEM((ROWS, TOK), f32),
            pltpu.VMEM((ROWS, TOK), f32),
            pltpu.SemaphoreType.DMA((copies,)),
            pltpu.SemaphoreType.DMA((copies,)),
            pltpu.SemaphoreType.DMA((BLOCKS + 5,)),
        ],
        compiler_params=pltpu.CompilerParams(
            collective_id=0, has_side_effects=True, vmem_limit_bytes=VMEM_ALL
        ),
        name="gather_project",
    )(tokens, *state, gate_weight.T)
    new_master, new_first, new_second, hidden = pl.pallas_call(
        head_kernel,
        out_shape=tuple(jax.ShapeDtypeStruct((COLS, CHUNK), f32) for _ in range(3))
        + (jax.ShapeDtypeStruct((TOK, QK), bf16),),
        in_specs=[vmem, vmem, smem, smem] + [hbm] * 4,
        out_specs=(hbm,) * 3 + (vmem,),
        scratch_shapes=[
            pltpu.VMEM((4, COLS, CHUNK), f32),
            pltpu.VMEM((3, COLS, CHUNK), f32),
            pltpu.SemaphoreType.DMA((7,)),
        ],
        compiler_params=pltpu.CompilerParams(vmem_limit_bytes=VMEM_ALL),
        name="head",
    )(projected, gates, input_bias, forget_bias, *state)
    return new_master.T, new_first.T, new_second.T, hidden


def solution(mesh):
    placed = (
        P(("group", "inner"), None),
        P("inner", "group"),
        P("inner", "group"),
        P("inner", "group"),
        P("inner", "group"),
        P("inner", None),
        P(),
        P(),
    )
    return jax.shard_map(
        on_device,
        mesh=mesh,
        in_specs=placed,
        out_specs=(
            P("inner", "group"),
            P("inner", "group"),
            P("inner", "group"),
            P(("group", "inner"), None),
        ),
        check_vma=False,
    )
```

time: 431 us -> 77.6 us (0.18)
  blocking collectives: 299 us -> 0 us
  waiting for transfers between devices: 104 us -> 0 us
  Pallas kernels: 0 us -> 75.3 us
  between operations: 15.4 us -> 1.93 us
  matrix products: 7.81 us -> 0 us
    all_gather x2 -> x0, blocking collectives: 299 us -> none  [the longest x1 225 us: on_device(): secondary = lax.all_gather(sendable, 'group', axis=1, tiled=True)]
    all_gather x1 -> x0, waiting for transfers between devices: 104 us -> none  [on_device(): lax.all_gather(secondary, 'inner', axis=0, tiled=True)]
    pallas_call x0 -> x2, Pallas kernels: none -> 75.3 us  [the longest x1 71.3 us: on_device(): pl.pallas_call(gather_kernel, out_shape=(jax.ShapeDtypeStruct((3 * QK, TO...]
    dot_general x4 -> x0, matrix products: 7.81 us -> none  [the longest x1 5.59 us: on_device(): jnp.dot(tokens, lax.all_gather(secondary, 'inner', axis=0, tiled=True), p...]
  transfers between devices with their start and end apart: 1 -> 0, of which waited for: 1 -> 0; matrix products, arithmetic and copies ran while one was open for 0% -> 0% of each run, Pallas kernels for 0% -> 0%
where the time goes in v1:
time: 77.6 us; the launch traced here: 77.3 us
  Pallas kernels  75.3 us (97%)
  between operations  1.93 us (2%)
    pallas_call x1, Pallas kernels, on_device(): pl.pallas_call(gather_kernel, out_shape=(jax.ShapeDtypeStruct((3 * QK, TO...  71.3 us
    pallas_call x1, Pallas kernels, on_device(): pl.pallas_call(head_kernel, out_shape=tuple((jax.ShapeDtypeStruct((COLS,...  3.99 us

profile of v1, /device:TPU:1, one launch (start us, length us, event | category | flops | bytes accessed | tf_op | source)
XLA Modules:
  0.0 77.3 jit_solution(7230326598233424438)
XLA Ops:
  1.9 71.3 %gather_project.1 = (bf16[768,384]{1,0:T(8,128)(2,1)}, f32[8,384]{1,0:T(8,128)}) custom-call(bf16[384,4096]{1,0:T(8,128)(2,1)} %tokens.1, f32[12,256]{1,0:T(8,128)} %bitcast.8, f32[12,256]{1,0:T(8,128)} %bitcast.10, f32[12,256]{1,0:T(8,128)} %bitcast.12, f32[12,256]{1,0:T(8,128)} %bitcast.14, bf16[2,256]{1,0:T(2,128)(2,1)} %bitcast.16), custom_call_target="tpu_custom_call" | custom-call | tf_op jit(solution)/shard_map/gather_project/pallas_call | solution.py:377
  73.3 4.0 %head.1 = (f32[12,256]{1,0:T(8,128)}, f32[12,256]{1,0:T(8,128)}, f32[12,256]{1,0:T(8,128)}, bf16[384,256]{1,0:T(8,128)(2,1)}) custom-call(bf16[768,384]{1,0:T(8,128)(2,1)} %get-tuple-element.10.projected, f32[8,384]{1,0:T(8,128)} %get-tuple-element.11.gates, f32[1]{0:T(128)S(6)} %copy.12.input_bias, f32[1]{0:T(128)S(6)} %copy.13.forget_bias, ...), custom_call_target="tpu_custom_call" | custom-call | tf_op jit(solution)/shard_map/head/pallas_call | solution.py:406

commit v2 on v1

v2 whole, which is shorter than its diff:
```python
import functools

import jax
import jax.numpy as jnp
from jax import lax
from jax.experimental import pallas as pl
from jax.experimental.pallas import tpu as pltpu
from jax.sharding import PartitionSpec as P

MESH = pl.DeviceIdType.MESH

QK = 256
NX, NY, NZL, NZH = 4, 8, 8, 2
NZ = NZL * NZH
REACH = 4
TOK = 384
CHUNK = 256
HALF = 128
COLS = 12
BLOCKS = NX * NZH * 2
ROWS_A = NY * NZL * 8
ROWS_B = NZL * NY * 4
ROWS_G = 16

VMEM_ALL = 67_043_328

beta_first = 0.9
beta_second = 0.999
learn_rate = 0.001
adam_eps = 1e-08
fix_first = 1.0 - (0.9**10) ** 10
fix_second = 1.0 - (0.999**10) ** 10

NT = (((1,), (1,)), ((), ()))


def adam(master, first, second, gradient):
    new_first = beta_first * first + (1.0 - beta_first) * gradient
    new_second = beta_second * second + (1.0 - beta_second) * gradient * gradient
    new_master = master - learn_rate * (new_first / fix_first) / (
        jnp.sqrt(new_second / fix_second) + adam_eps
    )
    return new_master, new_first, new_second


def gather_kernel(
    tokens,
    master,
    first,
    second,
    gradient,
    gate,
    out,
    gate_out,
    state,
    gate_in,
    x,
    pa,
    y1,
    pb,
    pg,
    gate_far,
    wt,
    a_rows,
    b_rows,
    g_rows,
    a_give,
    b_give,
    g_give,
    send_sem,
    recv_sem,
    local_sem,
):
    group, inner = lax.axis_index("group"), lax.axis_index("inner")
    zl, y = group // NY, group % NY
    xc, zh, core = inner // 4, (inner // 2) % 2, inner % 2
    z = zh * NZL + zl
    here = (xc, zh, y, zl)

    def device(x_=xc, y_=y, z_=z, core_=core):
        return ((z_ % NZL) * NY + y_, x_ * 4 + (z_ // NZL) * 2 + core_)

    def at_x(r):
        return device(x_=(xc + r + NX) % NX)

    def at_y(r):
        return device(y_=(y + r + NY) % NY)

    def at_z(r):
        return device(z_=(z + r + NZ) % NZ)

    other = device(core_=1 - core)

    loads = [
        pltpu.make_async_copy(src, dst, local_sem.at[1 + k])
        for k, (src, dst) in enumerate(
            [(ref, state.at[k]) for k, ref in enumerate((master, first, second, gradient))]
            + [(gate, gate_in)]
        )
    ]
    for c in loads:
        c.start()
    own_tokens = pltpu.make_async_copy(tokens, x.at[pl.ds(0, TOK)], local_sem.at[0])
    own_tokens.start()

    barrier = pltpu.get_barrier_semaphore()
    peers = (
        [at_z(sign * r) for r in range(1, REACH + 1) for sign in (1, -1)]
        + [at_y(r) for r in range(1, NY)]
        + [at_x(r) for r in range(1, NX)]
        + [other]
    )
    for peer in peers:
        pl.semaphore_signal(barrier, inc=1, device_id=peer, device_id_type=MESH)

    for c in loads:
        c.wait()
    new_master, _, _ = adam(state[0], state[1], state[2], state[3])
    pa[(0, *here, core)] = new_master[0:8, 0:HALF].astype(jnp.bfloat16)
    pa[(1, *here, core)] = new_master[0:8, HALF:].astype(jnp.bfloat16)
    y1[y, core] = jnp.concatenate(
        [new_master[8:12, 0:HALF], new_master[8:12, HALF:]], axis=0
    ).astype(jnp.bfloat16)
    gate_rows = jnp.concatenate(
        [gate_in[...].astype(jnp.float32), jnp.zeros((ROWS_G - 2, CHUNK), jnp.float32)], axis=0
    ).astype(jnp.bfloat16)
    pg[xc, core, 0] = gate_rows[:, 0:HALF]
    pg[xc, core, 1] = gate_rows[:, HALF:]

    pl.semaphore_wait(barrier, len(peers))

    a_tiles = (pa.at[(slice(0, 2), *here, 1)],) * 2
    b_tile = (y1.at[y, 0],) * 2
    g_tile = (pg.at[xc, 0],) * 2
    all_tokens = (tokens, x.at[pl.ds(TOK, TOK)])
    a_parts = [
        (a_give.at[pl.ds(k * 32, 32)], a_rows.at[pl.ds(k * 32, 32)]) for k in range(2)
    ]
    b_part, g_part = (b_give, b_rows), (g_give, g_rows)
    across = [a_tiles, b_tile, g_tile, all_tokens, *a_parts, b_part, g_part]

    def cross(pair):
        k = [p is pair for p in across].index(True)
        return pltpu.make_async_remote_copy(
            src_ref=pair[0],
            dst_ref=pair[1],
            send_sem=send_sem.at[k],
            recv_sem=recv_sem.at[k],
            device_id=other,
            device_id_type=MESH,
        )

    class Plan:
        def __init__(self):
            self.used, self.started = len(across), []

        def go(self, src, dev, dst=None):
            k = self.used
            self.used += 1
            c = pltpu.make_async_remote_copy(
                src_ref=src,
                dst_ref=src if dst is None else dst,
                send_sem=send_sem.at[k],
                recv_sem=recv_sem.at[k],
                device_id=dev,
                device_id_type=MESH,
            )
            c.start()
            self.started.append(c)
            return c

        def give(self, pair):
            c = cross(pair)
            c.start()
            self.started.append(c)

    def ring(go, count, chunks, region, coord, neighbour):
        half = count // 2
        copies = {}

        def begin(parts):
            for k in parts:
                for sign in (1, -1):
                    copies[sign, 1, k] = go(region(coord, k), neighbour(sign))

        def advance(step, k):
            for sign in (1, -1):
                if (sign, step, k) in copies:
                    copies[sign, step, k].wait_recv()
                    last = step + 1 == half
                    if step < half and (not last or (k < chunks // 2) == (sign > 0)):
                        block = (coord - sign * step + count) % count
                        copies[sign, step + 1, k] = go(region(block, k), neighbour(sign))

        return begin, advance

    def run(events):
        for _, event in sorted(events, key=lambda e: e[0]):
            event()

    @pl.when(core == 0)
    def _():
        plan = Plan()
        go = plan.go
        plan.give(b_tile)
        plan.give(g_tile)
        cross(a_tiles).wait_recv()

        def tile(slots, block):
            return pa.at[slots, xc, block // NZL, y, block % NZL]

        both = slice(0, 2)
        along_x, along_y = [], []

        def spread_x(block):
            along_x.extend(go(tile(0, block), at_x(r)) for r in (2, 1, 3))

        def spread_y(block):
            along_y.extend(go(tile(1, block), at_y(r)) for r in (4, 3, 5, 2, 6, 1, 7))

        a_z = {}
        for r in range(REACH, 0, -1):
            for sign in (1, -1):
                a_z[sign, r] = go(tile(both, z), at_z(sign * r))
        spread_y(z)
        spread_x(z)
        plan.give(all_tokens)
        for r in range(1, 2 * REACH + 1):
            for sign in (1, -1):
                block = (z - sign * r + NZ) % NZ
                a_z[sign, r].wait_recv()
                if r <= REACH:
                    slots = both if r < REACH else slice(0, 1) if sign > 0 else slice(1, 2)
                    a_z[sign, REACH + r] = go(tile(slots, block), at_z(sign * REACH))
                if r < 2 * REACH or sign < 0:
                    spread_y(block)
                if r < 2 * REACH or sign > 0:
                    spread_x(block)

        y_begin, y_step = ring(go, NY, NX, lambda b, k: pa.at[0, k, :, b], y, at_y)
        x_begin, x_step = ring(
            go, NX, 8, lambda b, k: pa.at[1, b, k // 4, pl.ds(2 * (k % 4), 2)], xc, at_x
        )

        def start(copies, begin, chunks):
            for c in copies:
                c.wait_recv()
            begin(range(chunks))

        events = [
            (13.6, lambda: start(along_x, y_begin, NX)),
            (15.6, lambda: start(along_y, x_begin, 8)),
        ]
        for step in range(1, NY // 2 + 1):
            for k in range(NX):
                events.append((16.3 + 2.8 * (step - 1) + 0.7 * k, functools.partial(y_step, step, k)))
        for step in range(1, NX // 2 + 1):
            for k in range(8):
                when = 18.5 + 5.6 * (step - 1) + 0.7 * (k if step == 1 else k % 4)
                events.append((when, functools.partial(x_step, step, k)))
        run(events)

        own_tokens.wait()
        cross(all_tokens).wait_recv()
        for block in range(BLOCKS):
            mx, mz, parity = block // 4, (block // 2) % 2, block % 2
            for kh in range(2):
                lanes = pl.ds(block * CHUNK + kh * HALF, HALF)
                wt[:, lanes] = pa[kh, mx, mz, :, :, parity].reshape(ROWS_A, HALF)
        for k in range(2):
            res = lax.dot_general(
                wt[k * 256 : (k + 1) * 256], x[...], NT, preferred_element_type=jnp.float32
            )
            res = res.reshape(32, 8, 2 * TOK).astype(jnp.bfloat16)
            a_give[k * 32 : (k + 1) * 32] = res[:, :, TOK:]
            plan.give(a_parts[k])
            a_rows[k * 32 : (k + 1) * 32] = res[:, :, :TOK]
        cross(g_part).wait_recv()
        cross(b_part).wait_recv()
        for c in plan.started:
            c.wait_send()

    @pl.when(core == 1)
    def _():
        plan = Plan()
        go = plan.go
        plan.give(a_tiles)
        cross(b_tile).wait_recv()
        b_y = [go(y1.at[y], at_y(r)) for r in (4, 3, 5, 2, 6, 1, 7)]
        cross(g_tile).wait_recv()
        g_x = [go(pg.at[xc], at_x(r)) for r in (2, 1, 3)]
        plan.give(all_tokens)
        for c in b_y:
            c.wait_recv()
        upper = lax.broadcasted_iota(jnp.int32, (8, HALF), 0) < 4
        for parity in range(2):
            low, high = [], []
            for a in range(NY // 2):
                even = y1[2 * a, parity].astype(jnp.float32)
                odd = y1[2 * a + 1, parity].astype(jnp.float32)
                low.append(jnp.where(upper, even, pltpu.roll(odd, 4, 0)))
                high.append(jnp.where(upper, pltpu.roll(even, 4, 0), odd))
            pb[xc, zh, zl, parity, 0] = jnp.concatenate(low, axis=0).astype(jnp.bfloat16)
            pb[xc, zh, zl, parity, 1] = jnp.concatenate(high, axis=0).astype(jnp.bfloat16)
        for c in g_x:
            c.wait_recv()
        b_x = [go(pb.at[xc, zh, zl], at_x(r)) for r in (1, 3, 2)]
        begin, step_of = ring(
            go, NZ, NX, lambda b, k: pb.at[(xc + k) % NX, b // NZL, b % NZL], z, at_z
        )
        begin((0,))
        g_z = [
            go(pg, at_z(sign * REACH), gate_far.at[k]) for k, sign in ((0, 1), (1, -1))
        ]

        def start(c, k):
            c.wait_recv()
            begin((k,))

        events = [
            (2.5, lambda: start(b_x[0], 3)),
            (2.6, lambda: start(b_x[1], 1)),
            (3.6, lambda: start(b_x[2], 2)),
        ]
        for step in range(1, NZ // 2 + 1):
            for k, late in ((0, 0.3), (1, 2.9), (3, 3.2), (2, 4.2)):
                events.append((late + 2.4 * step, functools.partial(step_of, step, k)))
        run(events)

        for c in g_z:
            c.wait_recv()
        for block in range(BLOCKS):
            mx, mz, parity = block // 4, (block // 2) % 2, block % 2
            for kh in range(2):
                lanes = pl.ds(block * CHUNK + kh * HALF, HALF)
                wt[0:ROWS_B, lanes] = pb[mx, mz, :, parity, kh].reshape(ROWS_B, HALF)
        for mx in range(NX):
            for parity in range(2):
                for kh in range(2):
                    near = (4 * mx + 2 * zh + parity) * CHUNK + kh * HALF
                    far = (4 * mx + 2 * (1 - zh) + parity) * CHUNK + kh * HALF
                    rows = pl.ds(ROWS_B, ROWS_G)
                    wt[rows, pl.ds(pl.multiple_of(near, HALF), HALF)] = pg[mx, parity, kh]
                    wt[rows, pl.ds(pl.multiple_of(far, HALF), HALF)] = gate_far[
                        zl // REACH, mx, parity, kh
                    ]
        own_tokens.wait()
        cross(all_tokens).wait_recv()
        res = lax.dot_general(
            wt[0 : ROWS_B + ROWS_G], x[...], NT, preferred_element_type=jnp.float32
        )
        g_rows[...] = res[ROWS_B:, :TOK]
        g_give[...] = res[ROWS_B:, TOK:]
        plan.give(g_part)
        res = res[:ROWS_B].reshape(32, 8, 2 * TOK).astype(jnp.bfloat16)
        b_give[...] = res[:, :, TOK:]
        plan.give(b_part)
        b_rows[...] = res[:, :, :TOK]
        for pair in a_parts:
            cross(pair).wait_recv()
        for c in plan.started:
            c.wait_send()

    gate_out[...] = g_rows[0:8]
    first4 = lax.broadcasted_iota(jnp.int32, (8, TOK), 0) < 4
    for l in range(NZL):
        rows = []
        for a in range(NY // 2):
            t0 = a_rows[2 * a * NZL + l].astype(jnp.float32)
            a1 = a_rows[(2 * a + 1) * NZL + l].astype(jnp.float32)
            b = b_rows[l * (NY // 2) + a].astype(jnp.float32)
            turned = pltpu.roll(a1, 4, 0)
            rows += [t0, jnp.where(first4, b, turned), jnp.where(first4, turned, b)]
        out[l * 96 : l * 96 + 96] = jnp.concatenate(rows, axis=0).astype(jnp.bfloat16)


def head_kernel(
    projected,
    gates,
    input_bias,
    forget_bias,
    master,
    first,
    second,
    gradient,
    new_master,
    new_first,
    new_second,
    hidden,
    state,
    updated,
    sems,
):
    loads = [
        pltpu.make_async_copy(ref, state.at[k], sems.at[k])
        for k, ref in enumerate((master, first, second, gradient))
    ]
    for c in loads:
        c.start()
    for c in loads:
        c.wait()
    updated[0], updated[1], updated[2] = adam(state[0], state[1], state[2], state[3])
    stores = [
        pltpu.make_async_copy(updated.at[k], ref, sems.at[4 + k])
        for k, ref in enumerate((new_master, new_first, new_second))
    ]
    for c in stores:
        c.start()
    pre = gates[...]
    input_gate = pre[0:1] + input_bias[0]
    forget = pre[1:2] + forget_bias[0]
    forget_log = jnp.minimum(forget, 0.0) - jnp.log1p(jnp.exp(-jnp.abs(forget)))
    t = lax.broadcasted_iota(jnp.int32, (TOK, TOK), 0)
    s = lax.broadcasted_iota(jnp.int32, (TOK, TOK), 1)
    causal = t >= s
    column = jnp.sum(jnp.where(causal, forget_log, 0.0), axis=1, keepdims=True)
    lane = lax.broadcasted_iota(jnp.int32, (8, TOK), 1)
    scan = jnp.broadcast_to(forget_log, (8, TOK))
    step = 1
    while step < TOK:
        scan = scan + jnp.where(lane >= step, pltpu.roll(scan, step, 1), 0.0)
        step *= 2
    row = scan[0:1]
    decay = jnp.exp(jnp.where(causal, column - row + input_gate, -jnp.inf))
    query = projected[0:QK].T
    scores = jnp.dot(query, projected[QK : 2 * QK], preferred_element_type=jnp.float32)
    weighted = scores * QK ** (-0.5) * decay
    normalizer = jnp.sum(weighted, axis=1, keepdims=True)
    numerator = lax.dot_general(
        weighted.astype(jnp.bfloat16),
        projected[2 * QK :],
        NT,
        preferred_element_type=jnp.float32,
    )
    hidden[...] = (numerator / jnp.maximum(jnp.abs(normalizer), 1.0)).astype(jnp.bfloat16)
    for c in stores:
        c.wait()


def on_device(
    tokens,
    master_weight,
    first_moment,
    second_moment,
    gradient,
    gate_weight,
    input_bias,
    forget_bias,
):
    state = [a.T for a in (master_weight, first_moment, second_moment, gradient)]
    vmem = pl.BlockSpec(memory_space=pltpu.VMEM)
    smem = pl.BlockSpec(memory_space=pltpu.SMEM)
    hbm = pl.BlockSpec(memory_space=pltpu.HBM)
    bf16, f32 = jnp.bfloat16, jnp.float32
    copies = 256
    projected, gates = pl.pallas_call(
        gather_kernel,
        out_shape=(
            jax.ShapeDtypeStruct((3 * QK, TOK), bf16),
            jax.ShapeDtypeStruct((8, TOK), f32),
        ),
        in_specs=[hbm] * 6,
        out_specs=(vmem, vmem),
        scratch_shapes=[
            pltpu.VMEM((4, COLS, CHUNK), f32),
            pltpu.VMEM((2, CHUNK), bf16),
            pltpu.VMEM((2 * TOK, BLOCKS * CHUNK), bf16),
            pltpu.VMEM((2, NX, NZH, NY, NZL, 2, 8, HALF), bf16),
            pltpu.VMEM((NY, 2, 8, HALF), bf16),
            pltpu.VMEM((NX, NZH, NZL, 2, 2, 32, HALF), bf16),
            pltpu.VMEM((NX, 2, 2, ROWS_G, HALF), bf16),
            pltpu.VMEM((2, NX, 2, 2, ROWS_G, HALF), bf16),
            pltpu.VMEM((ROWS_A, BLOCKS * CHUNK), bf16),
            pltpu.VMEM((64, 8, TOK), bf16),
            pltpu.VMEM((32, 8, TOK), bf16),
            pltpu.VMEM((ROWS_G, TOK), f32),
            pltpu.VMEM((64, 8, TOK), bf16),
            pltpu.VMEM((32, 8, TOK), bf16),
            pltpu.VMEM((ROWS_G, TOK), f32),
            pltpu.SemaphoreType.DMA((copies,)),
            pltpu.SemaphoreType.DMA((copies,)),
            pltpu.SemaphoreType.DMA((6,)),
        ],
        compiler_params=pltpu.CompilerParams(
            collective_id=0, has_side_effects=True, vmem_limit_bytes=VMEM_ALL
        ),
        name="gather_project",
    )(tokens, *state, gate_weight.T)
    new_master, new_first, new_second, hidden = pl.pallas_call(
        head_kernel,
        out_shape=tuple(jax.ShapeDtypeStruct((COLS, CHUNK), f32) for _ in range(3))
        + (jax.ShapeDtypeStruct((TOK, QK), bf16),),
        in_specs=[vmem, vmem, smem, smem] + [hbm] * 4,
        out_specs=(hbm,) * 3 + (vmem,),
        scratch_shapes=[
            pltpu.VMEM((4, COLS, CHUNK), f32),
            pltpu.VMEM((3, COLS, CHUNK), f32),
            pltpu.SemaphoreType.DMA((7,)),
        ],
        compiler_params=pltpu.CompilerParams(vmem_limit_bytes=VMEM_ALL),
        name="head",
    )(projected, gates, input_bias, forget_bias, *state)
    return new_master.T, new_first.T, new_second.T, hidden


def solution(mesh):
    placed = (
        P(("group", "inner"), None),
        P("inner", "group"),
        P("inner", "group"),
        P("inner", "group"),
        P("inner", "group"),
        P("inner", None),
        P(),
        P(),
    )
    return jax.shard_map(
        on_device,
        mesh=mesh,
        in_specs=placed,
        out_specs=(
            P("inner", "group"),
            P("inner", "group"),
            P("inner", "group"),
            P(("group", "inner"), None),
        ),
        check_vma=False,
    )
```

time: 77.6 us -> 71.1 us (0.916)
  Pallas kernels: 75.3 us -> 68.8 us
    pallas_call x1, Pallas kernels: 71.3 us -> 64.9 us  [on_device(): pl.pallas_call(gather_kernel, out_shape=(jax.ShapeDtypeStruct((3 * QK, TO...]
where the time goes in v2:
time: 71.1 us; the launch traced here: 70.8 us
  Pallas kernels  68.8 us (97%)
  between operations  1.93 us (3%)
    pallas_call x1, Pallas kernels, on_device(): pl.pallas_call(gather_kernel, out_shape=(jax.ShapeDtypeStruct((3 * QK, TO...  64.9 us
    pallas_call x1, Pallas kernels, on_device(): pl.pallas_call(head_kernel, out_shape=tuple((jax.ShapeDtypeStruct((COLS,...  3.99 us

profile of v2, /device:TPU:1, one launch (start us, length us, event | category | flops | bytes accessed | tf_op | source)
XLA Modules:
  0.0 70.8 jit_solution(4045520537043573196)
XLA Ops:
  1.9 64.9 %gather_project.1 = (bf16[768,384]{1,0:T(8,128)(2,1)}, f32[8,384]{1,0:T(8,128)}) custom-call(bf16[384,4096]{1,0:T(8,128)(2,1)} %tokens.1, f32[12,256]{1,0:T(8,128)} %bitcast.8, f32[12,256]{1,0:T(8,128)} %bitcast.10, f32[12,256]{1,0:T(8,128)} %bitcast.12, f32[12,256]{1,0:T(8,128)} %bitcast.14, bf16[2,256]{1,0:T(2,128)(2,1)} %bitcast.16), custom_call_target="tpu_custom_call" | custom-call | tf_op jit(solution)/shard_map/gather_project/pallas_call | solution.py:456
  66.8 4.0 %head.1 = (f32[12,256]{1,0:T(8,128)}, f32[12,256]{1,0:T(8,128)}, f32[12,256]{1,0:T(8,128)}, bf16[384,256]{1,0:T(8,128)(2,1)}) custom-call(bf16[768,384]{1,0:T(8,128)(2,1)} %get-tuple-element.10.projected, f32[8,384]{1,0:T(8,128)} %get-tuple-element.11.gates, f32[1]{0:T(128)S(6)} %copy.12.input_bias, f32[1]{0:T(128)S(6)} %copy.13.forget_bias, ...), custom_call_target="tpu_custom_call" | custom-call | tf_op jit(solution)/shard_map/head/pallas_call | solution.py:489

commit v3 on v2

--- a/solution.py
+++ b/solution.py
@@ -16,6 +16,7 @@
 TOK = 384
 CHUNK = 256
 HALF = 128
+FULL = 512
 COLS = 12
 BLOCKS = NX * NZH * 2
 ROWS_A = NY * NZL * 8
@@ -100,7 +101,7 @@
     ]
     for c in loads:
         c.start()
-    own_tokens = pltpu.make_async_copy(tokens, x.at[pl.ds(0, TOK)], local_sem.at[0])
+    own_tokens = pltpu.make_async_copy(tokens, x.at[pl.ds(TOK, TOK)], local_sem.at[0])
     own_tokens.start()
 
     barrier = pltpu.get_barrier_semaphore()
@@ -132,7 +133,7 @@
     a_tiles = (pa.at[(slice(0, 2), *here, 1)],) * 2
     b_tile = (y1.at[y, 0],) * 2
     g_tile = (pg.at[xc, 0],) * 2
-    all_tokens = (tokens, x.at[pl.ds(TOK, TOK)])
+    all_tokens = (tokens, x.at[pl.ds(0, TOK)])
     a_parts = [
         (a_give.at[pl.ds(k * 32, 32)], a_rows.at[pl.ds(k * 32, 32)]) for k in range(2)
     ]
@@ -174,7 +175,7 @@
             c.start()
             self.started.append(c)
 
-    def ring(go, count, chunks, region, coord, neighbour):
+    def ring(go, count, chunks, region, coord, neighbour, landed):
         half = count // 2
         copies = {}
 
@@ -182,15 +183,21 @@
             for k in parts:
                 for sign in (1, -1):
                     copies[sign, 1, k] = go(region(coord, k), neighbour(sign))
+            for k in parts:
+                landed(coord, k)
 
         def advance(step, k):
+            blocks = []
             for sign in (1, -1):
                 if (sign, step, k) in copies:
                     copies[sign, step, k].wait_recv()
                     last = step + 1 == half
+                    block = (coord - sign * step + count) % count
+                    blocks.append(block)
                     if step < half and (not last or (k < chunks // 2) == (sign > 0)):
-                        block = (coord - sign * step + count) % count
                         copies[sign, step + 1, k] = go(region(block, k), neighbour(sign))
+            for block in blocks:
+                landed(block, k)
 
         return begin, advance
 
@@ -237,9 +244,32 @@
                 if r < 2 * REACH or sign > 0:
                     spread_x(block)
 
-        y_begin, y_step = ring(go, NY, NX, lambda b, k: pa.at[0, k, :, b], y, at_y)
+        def landed_y(b, k):
+            rows = pl.ds(pl.multiple_of(b * 64, 64), 64)
+            for far in range(NZH):
+                for parity in range(2):
+                    lanes = pl.ds((4 * k + 2 * far + parity) * CHUNK, HALF)
+                    wt[rows, lanes] = pa[0, k, far, b, :, parity].reshape(64, HALF)
+
+        def landed_x(b, k):
+            far, top = k // 4, 2 * (k % 4)
+            for parity in range(2):
+                lane = pl.multiple_of((4 * b + 2 * far + parity) * CHUNK + HALF, HALF)
+                wt[top * 64 : top * 64 + 128, pl.ds(lane, HALF)] = jnp.concatenate(
+                    [pa[1, b, far, top + n, :, parity].reshape(64, HALF) for n in range(2)], axis=0
+                )
+
+        y_begin, y_step = ring(
+            go, NY, NX, lambda b, k: pa.at[0, k, :, b], y, at_y, landed_y
+        )
         x_begin, x_step = ring(
-            go, NX, 8, lambda b, k: pa.at[1, b, k // 4, pl.ds(2 * (k % 4), 2)], xc, at_x
+            go,
+            NX,
+            8,
+            lambda b, k: pa.at[1, b, k // 4, pl.ds(2 * (k % 4), 2)],
+            xc,
+            at_x,
+            landed_x,
         )
 
         def start(copies, begin, chunks):
@@ -262,19 +292,21 @@
 
         own_tokens.wait()
         cross(all_tokens).wait_recv()
-        for block in range(BLOCKS):
-            mx, mz, parity = block // 4, (block // 2) % 2, block % 2
-            for kh in range(2):
-                lanes = pl.ds(block * CHUNK + kh * HALF, HALF)
-                wt[:, lanes] = pa[kh, mx, mz, :, :, parity].reshape(ROWS_A, HALF)
         for k in range(2):
             res = lax.dot_general(
-                wt[k * 256 : (k + 1) * 256], x[...], NT, preferred_element_type=jnp.float32
+                wt[k * 256 : (k + 1) * 256], x[0:FULL], NT, preferred_element_type=jnp.float32
             )
-            res = res.reshape(32, 8, 2 * TOK).astype(jnp.bfloat16)
-            a_give[k * 32 : (k + 1) * 32] = res[:, :, TOK:]
+            res = res.reshape(32, 8, FULL).astype(jnp.bfloat16)
+            a_give[k * 32 : (k + 1) * 32] = res[:, :, :TOK]
             plan.give(a_parts[k])
-            a_rows[k * 32 : (k + 1) * 32] = res[:, :, :TOK]
+            a_rows[k * 32 : (k + 1) * 32, :, 0 : FULL - TOK] = res[:, :, TOK:]
+        for k in range(2):
+            res = lax.dot_general(
+                wt[k * 256 : (k + 1) * 256], x[FULL:], NT, preferred_element_type=jnp.float32
+            )
+            a_rows[k * 32 : (k + 1) * 32, :, FULL - TOK :] = res.reshape(
+                32, 8, 2 * TOK - FULL
+            ).astype(jnp.bfloat16)
         cross(g_part).wait_recv()
         cross(b_part).wait_recv()
         for c in plan.started:
@@ -305,8 +337,25 @@
         for c in g_x:
             c.wait_recv()
         b_x = [go(pb.at[xc, zh, zl], at_x(r)) for r in (1, 3, 2)]
+
+        def landed_z(b, k):
+            mx, far, low_z = (xc + k) % NX, b // NZL, b % NZL
+            rows = pl.ds(pl.multiple_of(low_z * 32, 32), 32)
+            for parity in range(2):
+                for kh in range(2):
+                    lane = (4 * mx + 2 * far + parity) * CHUNK + kh * HALF
+                    wt[rows, pl.ds(pl.multiple_of(lane, HALF), HALF)] = pb[
+                        mx, far, low_z, parity, kh
+                    ]
+
         begin, step_of = ring(
-            go, NZ, NX, lambda b, k: pb.at[(xc + k) % NX, b // NZL, b % NZL], z, at_z
+            go,
+            NZ,
+            NX,
+            lambda b, k: pb.at[(xc + k) % NX, b // NZL, b % NZL],
+            z,
+            at_z,
+            landed_z,
         )
         begin((0,))
         g_z = [
@@ -329,11 +378,6 @@
 
         for c in g_z:
             c.wait_recv()
-        for block in range(BLOCKS):
-            mx, mz, parity = block // 4, (block // 2) % 2, block % 2
-            for kh in range(2):
-                lanes = pl.ds(block * CHUNK + kh * HALF, HALF)
-                wt[0:ROWS_B, lanes] = pb[mx, mz, :, parity, kh].reshape(ROWS_B, HALF)
         for mx in range(NX):
             for parity in range(2):
                 for kh in range(2):
@@ -347,15 +391,22 @@
         own_tokens.wait()
         cross(all_tokens).wait_recv()
         res = lax.dot_general(
-            wt[0 : ROWS_B + ROWS_G], x[...], NT, preferred_element_type=jnp.float32
-        )
-        g_rows[...] = res[ROWS_B:, :TOK]
-        g_give[...] = res[ROWS_B:, TOK:]
+            wt[0 : ROWS_B + ROWS_G], x[0:FULL], NT, preferred_element_type=jnp.float32
+        )
+        rows = res[:ROWS_B].reshape(32, 8, FULL).astype(jnp.bfloat16)
+        b_give[...] = rows[:, :, :TOK]
+        plan.give(b_part)
+        g_give[...] = res[ROWS_B:, :TOK]
         plan.give(g_part)
-        res = res[:ROWS_B].reshape(32, 8, 2 * TOK).astype(jnp.bfloat16)
-        b_give[...] = res[:, :, TOK:]
-        plan.give(b_part)
-        b_rows[...] = res[:, :, :TOK]
+        b_rows[:, :, 0 : FULL - TOK] = rows[:, :, TOK:]
+        g_rows[:, 0 : FULL - TOK] = res[ROWS_B:, TOK:]
+        res = lax.dot_general(
+            wt[0 : ROWS_B + ROWS_G], x[FULL:], NT, preferred_element_type=jnp.float32
+        )
+        b_rows[:, :, FULL - TOK :] = (
+            res[:ROWS_B].reshape(32, 8, 2 * TOK - FULL).astype(jnp.bfloat16)
+        )
+        g_rows[:, FULL - TOK :] = res[ROWS_B:]
         for pair in a_parts:
             cross(pair).wait_recv()
         for c in plan.started:

time: 71.1 us -> 69.2 us (0.973)
  Pallas kernels: 68.8 us -> 66.9 us
    pallas_call x1, Pallas kernels: 64.9 us -> 62.9 us  [on_device(): pl.pallas_call(gather_kernel, out_shape=(jax.ShapeDtypeStruct((3 * QK, TO...]
where the time goes in v3:
time: 69.2 us; the launch traced here: 68.9 us
  Pallas kernels  66.9 us (97%)
  between operations  1.93 us (3%)
    pallas_call x1, Pallas kernels, on_device(): pl.pallas_call(gather_kernel, out_shape=(jax.ShapeDtypeStruct((3 * QK, TO...  62.9 us
    pallas_call x1, Pallas kernels, on_device(): pl.pallas_call(head_kernel, out_shape=tuple((jax.ShapeDtypeStruct((COLS,...  3.98 us

profile of v3, /device:TPU:1, one launch (start us, length us, event | category | flops | bytes accessed | tf_op | source)
XLA Modules:
  0.0 68.9 jit_solution(15043642516251308213)
XLA Ops:
  1.9 62.9 %gather_project.1 = (bf16[768,384]{1,0:T(8,128)(2,1)}, f32[8,384]{1,0:T(8,128)}) custom-call(bf16[384,4096]{1,0:T(8,128)(2,1)} %tokens.1, f32[12,256]{1,0:T(8,128)} %bitcast.8, f32[12,256]{1,0:T(8,128)} %bitcast.10, f32[12,256]{1,0:T(8,128)} %bitcast.12, f32[12,256]{1,0:T(8,128)} %bitcast.14, bf16[2,256]{1,0:T(2,128)(2,1)} %bitcast.16), custom_call_target="tpu_custom_call" | custom-call | tf_op jit(solution)/shard_map/gather_project/pallas_call | solution.py:507
  64.9 4.0 %head.1 = (f32[12,256]{1,0:T(8,128)}, f32[12,256]{1,0:T(8,128)}, f32[12,256]{1,0:T(8,128)}, bf16[384,256]{1,0:T(8,128)(2,1)}) custom-call(bf16[768,384]{1,0:T(8,128)(2,1)} %get-tuple-element.10.projected, f32[8,384]{1,0:T(8,128)} %get-tuple-element.11.gates, f32[1]{0:T(128)S(6)} %copy.12.input_bias, f32[1]{0:T(128)S(6)} %copy.13.forget_bias, ...), custom_call_target="tpu_custom_call" | custom-call | tf_op jit(solution)/shard_map/head/pallas_call | solution.py:540
